TPU v7x, 128 devices: a whole 4x4x4 slice. The times are simulated.
128 devices in a mesh: shot: 8 (over x, z_hi), dom: 16 (over z_lo, y, core).
Axes of the slice: x: 4, y: 4, z: 4 (z_hi: 2, z_lo: 2; z = z_hi * 2 + z_lo), core: 2. Of those that a mesh axis runs over, the one named last changes fastest.
Arguments:
- velocity: float32 [512, 32, 128], P('dom'), may hold values from 1.5 to 3
- noise_field: float32 [512, 32, 128], P('dom'), may hold values from -6 to 6
- step_size: float32 [1], replicated, may hold values from 0.05 to 0.5
- field_prev: float32 [16, 512, 32, 128], P('shot', 'dom'), may hold values from -6 to 6
- field_now: float32 [16, 512, 32, 128], P('shot', 'dom'), may hold values from -6 to 6
- adjoint_next: float32 [16, 512, 32, 128], P('shot', 'dom'), may hold values from -6 to 6
- adjoint_now: float32 [16, 512, 32, 128], P('shot', 'dom'), may hold values from -6 to 6
- wavelet: float32 [16, 4], P('shot'), may hold values from -8 to 8
- source_cells: int32 [16, 8], P('shot'), may hold values from 0 to 2097151
- source_signs: int32 [16, 8], P('shot'), may hold values from 0 to 1
- record_cells: int32 [16, 256], P('shot'), may hold values from 0 to 2097151
- observed: float32 [16, 4, 256], P('shot'), may hold values from -6 to 6
Outputs:
- new_velocity: float32 [512, 32, 128], P('dom', None, 'shot')
Inputs may be any that keep to these rules, and one draw needn't show every extreme that they name: `source_signs`: 0 stands for a negative sign, 1 for a positive one. `source_cells`: cells flattened as x 32 * 128 + z * 128 + y. `record_cells`: cells flattened as x 32 * 128 + z * 128 + y.
All inputs are finite; a program needn't handle non-finite values.
Results may differ from a plain program's by a relative error of at most 0.00009.
Values sent between devices are 32-bit elements; how exact they have to be, the bound alone decides.
No kernel may reach another device: no remote copies, remote signals or barrier semaphores. Data moves between devices by JAX's collectives and lax.ppermute only.
A program may use at most 128 MiB of HBM per device.

v0:
```python
import math
import jax
import jax.numpy as jnp
from jax import lax
from jax.sharding import PartitionSpec as P

STEPS = 4
COEFFS = (-205.0 / 72.0, 8.0 / 5.0, -1.0 / 5.0, 8.0 / 315.0, -1.0 / 560.0)
COURANT = 0.02


def extended(block, sides, width):
    for axis, dim in sides:
        count = lax.axis_size(axis)
        forward = [(i, i + 1) for i in range(count - 1)]
        backward = [(target, source) for source, target in forward]
        low = lax.ppermute(
            lax.slice_in_dim(block, block.shape[dim] - width, None, axis=dim), axis, forward
        )
        high = lax.ppermute(lax.slice_in_dim(block, 0, width, axis=dim), axis, backward)
        block = jnp.concatenate([low, block, high], axis=dim)
    return block


def stencil(padded):
    margin = 4
    rank = padded.ndim
    lengths = [padded.shape[rank - 3 + place] - 2 * margin for place in range(3)]

    def window(offsets):
        sliced = padded
        for place in range(3):
            begin = margin + offsets[place]
            sliced = lax.slice_in_dim(sliced, begin, begin + lengths[place], axis=rank - 3 + place)
        return sliced

    summed = 3.0 * COEFFS[0] * window((0, 0, 0))
    for distance in range(1, 5):
        beside_all = window((distance, 0, 0)) + window((-distance, 0, 0))
        beside_all = beside_all + window((0, distance, 0)) + window((0, -distance, 0))
        beside_all = beside_all + window((0, 0, distance)) + window((0, 0, -distance))
        summed = summed + COEFFS[distance] * beside_all
    return summed


def cosine_basis(length):
    wave_index = jnp.arange(length, dtype=jnp.int32)[:, None]
    position = jnp.arange(length, dtype=jnp.int32)[None, :]
    phase = wave_index * (2 * position + 1) % (4 * length)
    angle = math.pi / (2.0 * length) * phase.astype(jnp.float32)
    factor = jnp.where(wave_index == 0, math.sqrt(1.0 / length), math.sqrt(2.0 / length)).astype(
        jnp.float32
    )
    return factor * jnp.cos(angle)


def prior_gain(length, cutoff):
    scaled = jnp.arange(length, dtype=jnp.float32) / float(cutoff)
    return 1.0 / jnp.sqrt(1.0 + scaled)


def precondition(gradient, noise_cols, rate):
    length = gradient.shape[0]
    basis = cosine_basis(length)
    spectrum = prior_gain(length, length // 32)[:, None]
    highest = lax.Precision.HIGHEST
    grad_hat = jnp.dot(basis, gradient.reshape(length, -1), precision=highest)
    noise_hat = jnp.dot(basis, noise_cols.reshape(length, -1), precision=highest)
    weights = spectrum * (-0.5 * rate * spectrum * grad_hat + jnp.sqrt(rate) * noise_hat)
    update = lax.dot_general(basis, weights, (((0,), (0,)), ((), ())), precision=highest)
    return update.reshape(gradient.shape)


def widen(padded):
    return jnp.pad(padded, ((0, 0), (0, 0), (4, 4), (4, 4)))


def body(
    velocity,
    noise_field,
    step_size,
    field_prev,
    field_now,
    adjoint_next,
    adjoint_now,
    wavelet,
    source_cells,
    source_signs,
    record_cells,
    observed,
):
    speed_sq = COURANT * velocity * velocity
    shots_here = field_now.shape[0]
    slab_rows = velocity.shape[0]
    plane_cells = velocity.shape[1] * velocity.shape[2]
    slab_cells = slab_rows * plane_cells
    first_row = lax.axis_index("dom") * slab_rows
    offset = first_row * plane_cells
    row_ids = jnp.arange(shots_here, dtype=jnp.int32)[:, None]
    source_local = source_cells - offset
    source_inside = (source_local >= 0) & (source_local < slab_cells)
    source_target = jnp.where(source_inside, source_local, slab_cells)
    record_local = record_cells - offset
    record_inside = (record_local >= 0) & (record_local < slab_cells)
    record_target = jnp.where(record_inside, record_local, slab_cells)
    record_clip = jnp.clip(record_local, 0, slab_cells - 1)
    amplitude = (2 * source_signs - 1).astype(jnp.float32)

    def place(field, target, values):
        flat = field.reshape(shots_here, -1)
        rows_full = jnp.broadcast_to(row_ids, target.shape)
        return flat.at[rows_full, target].add(values, mode="drop").reshape(field.shape)

    summed = jnp.zeros(field_now.shape, jnp.float32)
    prior, current = (field_prev, field_now)
    laplacians = []
    samples = []
    for moment in range(STEPS):
        padded = extended(current, (("dom", 1),), 4)
        spread = stencil(widen(padded))
        laplacians.append(spread)
        advanced = 2.0 * current - prior + speed_sq * spread
        advanced = place(advanced, source_target, amplitude * wavelet[:, moment][:, None])
        samples.append(jnp.take_along_axis(advanced.reshape(shots_here, -1), record_clip, axis=1))
        prior, current = (current, advanced)
    adj_later, adj_current = (adjoint_next, adjoint_now)
    for moment in range(STEPS, 0, -1):
        misfit = samples[moment - 1] - observed[:, moment - 1, :]
        padded = extended(adj_current, (("dom", 1),), 4)
        spread = stencil(widen(padded))
        earlier = 2.0 * adj_current - adj_later + speed_sq * spread
        earlier = place(earlier, record_target, misfit)
        adj_later, adj_current = (adj_current, earlier)
        summed = summed + adj_current * laplacians[moment - 1]
    partial_value = 2.0 * COURANT * velocity * jnp.sum(summed, axis=0)
    rate = step_size[0]
    shot_rows = velocity.shape[2] // lax.axis_size("shot")
    start = lax.axis_index("shot") * shot_rows
    total = lax.psum(partial_value, "shot")
    grad_cols, noise_cols = (
        lax.all_to_all(total, "dom", split_axis=2, concat_axis=0, tiled=True),
        lax.all_to_all(noise_field, "dom", split_axis=2, concat_axis=0, tiled=True),
    )
    update = precondition(grad_cols, noise_cols, rate)
    returned = lax.all_to_all(update, "dom", split_axis=0, concat_axis=2, tiled=True)
    result = lax.dynamic_slice_in_dim(velocity + returned, start, shot_rows, 2)
    return result


def solution(mesh):
    placed = (
        P("dom", None, None),
        P("dom", None, None),
        P(),
        P("shot", "dom", None, None),
        P("shot", "dom", None, None),
        P("shot", "dom", None, None),
        P("shot", "dom", None, None),
        P("shot", None),
        P("shot", None),
        P("shot", None),
        P("shot", None),
        P("shot", None, None),
    )
    return jax.shard_map(
        body, mesh=mesh, in_specs=placed, out_specs=P("dom", None, "shot"), check_vma=False
    )
```

profile of v0, /device:TPU:1, one launch (start us, length us, event | category | flops | bytes accessed | tf_op | source)
XLA Modules:
  0.0 571.0 jit_solution(9023833268099805198)
XLA Ops:
  37.4 8.3 %multiply_add_fusion.3 = (f32[2,32,32,128]{3,2,1,0:T(8,128)}, f32[2,32,32,128]{3,2,1,0:T(8,128)}) fusion(f32[2,32,32,128]{3,2,1,0:T(8,128)} %param.17, f32[2,32,32,128]{3,2,1,0:T(8,128)} %param.18, f32[32,32,128]{2,1,0:T(8,128)} %multiply_multiply_fusion, f32[2,40,40,136]{3,2,1,0:T(8,128)S(1)} %select_maximum_fusion.12, f32[2,36,32,128]{3,2,1,0:T(8,128)} %copy-done.23, ...), kind=kLoop, calls=%fused_computation.293 | loop fusion | flops 8650752 | bytes 29884416 | tf_op jit(solution)/shard_map/add | solution.py:122
  66.2 22.5 %multiply_add_fusion.2 = (f32[2,32,32,128]{3,2,1,0:T(8,128)}, f32[2,32,32,128]{3,2,1,0:T(8,128)}) fusion(f32[2,32,32,128]{3,2,1,0:T(8,128)} %param.18, f32[2,32,32,128]{3,2,1,0:T(8,128)} %bitcast.179, f32[32,32,128]{2,1,0:T(8,128)} %multiply_multiply_fusion, f32[2,40,40,136]{3,2,1,0:T(8,128)} %select_maximum_fusion.10, ...), kind=kLoop, calls=%fused_computation.292 | loop fusion | flops 8650752 | bytes 29884416 | tf_op jit(solution)/shard_map/add | solution.py:122
  101.3 7.9 %fusion.75 = f32[2,32,32,128]{3,2,1,0:T(8,128)} fusion(f32[2,40,40,136]{3,2,1,0:T(8,128)S(1)} %select_maximum_fusion.14, f32[2,36,32,128]{3,2,1,0:T(8,128)} %copy-done.22, f32[2,36,32,128]{3,2,1,0:T(8,128)} %constant_dynamic-update-slice_fusion, f32[2,32,32,128]{3,2,1,0:T(8,128)S(1)} %copy-done.18, f32[2,32,32,128]{3,2,1,0:T(8,128)} %param.19, ...), kind=kLoop, calls=%fused_computation.263 | loop fusion | flops 8650752 | bytes 28835840 | tf_op jit(solution)/shard_map/add | solution.py:131
  112.4 4.8 gather_fusion.3
  127.4 8.2 %multiply_add_fusion.1 = (f32[2,32,32,128]{3,2,1,0:T(8,128)}, f32[2,32,32,128]{3,2,1,0:T(8,128)}) fusion(f32[2,32,32,128]{3,2,1,0:T(8,128)} %bitcast.180, f32[2,32,32,128]{3,2,1,0:T(8,128)} %bitcast.183, f32[32,32,128]{2,1,0:T(8,128)} %multiply_multiply_fusion, f32[2,40,40,136]{3,2,1,0:T(8,128)S(1)} %select_maximum_fusion.8, ...), kind=kLoop, calls=%fused_computation.291 | loop fusion | flops 8650752 | bytes 29884416 | tf_op jit(solution)/shard_map/add | solution.py:122
  142.4 7.1 %gather_fusion.2 = f32[512]{0:T(512)} fusion(f32[2,131072]{1,0:T(2,128)S(1)} %copy-done.16, s32[512]{0:T(512)S(1)} %bitcast.156), kind=kCustom, calls=%fused_computation.2.clone | custom fusion | bytes 8192 | tf_op jit(solution)/shard_map/jit(take_along_axis)/gather | solution.py:124
  165.1 8.2 %multiply_add_fusion = (f32[2,32,32,128]{3,2,1,0:T(8,128)}, f32[2,32,32,128]{3,2,1,0:T(8,128)}) fusion(f32[2,32,32,128]{3,2,1,0:T(8,128)} %bitcast.184, f32[2,32,32,128]{3,2,1,0:T(8,128)} %bitcast.195, f32[32,32,128]{2,1,0:T(8,128)} %multiply_multiply_fusion, f32[2,40,40,136]{3,2,1,0:T(8,128)S(1)} %select_maximum_fusion.6, ...), kind=kLoop, calls=%fused_computation.290 | loop fusion | flops 8650752 | bytes 29884416 | tf_op jit(solution)/shard_map/add | solution.py:122
  176.9 4.8 gather_fusion
  181.8 24.7 %scatter_fusion.4 = f32[2,131072]{1,0:T(2,128)S(1)} fusion(f32[2,131072]{1,0:T(2,128)S(1)} %bitcast.196, s32[512]{0:T(512)S(1)} %bitcast.151, f32[512]{0:T(512)S(1)} %bitcast.224), kind=kCustom, calls=%fused_computation.8 | custom fusion | flops 512 | bytes 10240 | tf_op jit(solution)/shard_map/scatter-add | solution.py:112
  219.1 7.8 %fusion.33 = f32[2,32,32,128]{3,2,1,0:T(8,128)} fusion(f32[2,40,40,136]{3,2,1,0:T(8,128)S(1)} %select_maximum_fusion.4, f32[2,36,32,128]{3,2,1,0:T(8,128)} %copy-done.26, f32[2,36,32,128]{3,2,1,0:T(8,128)} %constant_dynamic-update-slice_fusion.20, f32[2,32,32,128]{3,2,1,0:T(8,128)S(1)} %bitcast.162, f32[2,32,32,128]{3,2,1,0:T(8,128)} %param.20, ...), kind=kLoop, calls=%fused_computation.121 | loop fusion | flops 8650752 | bytes 28835840 | tf_op jit(solution)/shard_map/add | solution.py:131
  229.0 24.7 %scatter_fusion.5 = f32[2,131072]{1,0:T(2,128)S(1)} fusion(f32[2,131072]{1,0:T(2,128)S(1)} %bitcast.201, s32[512]{0:T(512)S(1)} %bitcast.152, f32[512]{0:T(512)S(1)} %bitcast.222), kind=kCustom, calls=%fused_computation.9 | custom fusion | flops 512 | bytes 10240 | tf_op jit(solution)/shard_map/scatter-add | solution.py:112
  260.9 7.2 %collective-permute-done.12 = f32[2,4,32,128]{3,2,1,0:T(8,128)S(1)} collective-permute-done((f32[2,4,32,128]{3,2,1,0:T(8,128)S(1)}, f32[2,4,32,128]{3,2,1,0:T(8,128)S(1)}, u32[]{:S(2)}, u32[]{:S(2)}) %collective-permute-start.12) | collective-permute-done | bytes 131104 | tf_op jit(solution)/shard_map/ppermute | solution.py:20
  270.3 7.8 %fusion.23 = f32[2,32,32,128]{3,2,1,0:T(8,128)} fusion(f32[2,40,40,136]{3,2,1,0:T(8,128)S(1)} %select_maximum_fusion.2, f32[2,36,32,128]{3,2,1,0:T(8,128)} %copy-done.27, f32[2,36,32,128]{3,2,1,0:T(8,128)} %constant_dynamic-update-slice_fusion.24, f32[2,32,32,128]{3,2,1,0:T(8,128)} %bitcast.168, f32[2,32,32,128]{3,2,1,0:T(8,128)S(1)} %bitcast.163, ...), kind=kLoop, calls=%fused_computation.91 | loop fusion | flops 8650752 | bytes 28835840 | tf_op jit(solution)/shard_map/add | solution.py:131
  280.1 24.7 %scatter_fusion.6 = f32[2,131072]{1,0:T(2,128)S(1)} fusion(f32[2,131072]{1,0:T(2,128)S(1)} %bitcast.203, s32[512]{0:T(512)S(1)} %bitcast.153, f32[512]{0:T(512)S(1)} %bitcast.223), kind=kCustom, calls=%fused_computation.10 | custom fusion | flops 512 | bytes 10240 | tf_op jit(solution)/shard_map/scatter-add | solution.py:112
  317.5 7.9 %fusion.13 = f32[2,32,32,128]{3,2,1,0:T(8,128)} fusion(f32[2,40,40,136]{3,2,1,0:T(8,128)S(1)} %select_maximum_fusion, f32[2,36,32,128]{3,2,1,0:T(8,128)} %copy-done.28, f32[2,36,32,128]{3,2,1,0:T(8,128)} %constant_dynamic-update-slice_fusion.28, f32[2,32,32,128]{3,2,1,0:T(8,128)} %bitcast.174, f32[2,32,32,128]{3,2,1,0:T(8,128)S(1)} %bitcast.169, ...), kind=kLoop, calls=%fused_computation.61 | loop fusion | flops 8650752 | bytes 28835840 | tf_op jit(solution)/shard_map/add | solution.py:131
  328.4 70.2 %scatter_fusion.7 = f32[2,131072]{1,0:T(2,128)} fusion(f32[2,131072]{1,0:T(2,128)} %bitcast.199, s32[512]{0:T(512)S(1)} %bitcast.154, f32[512]{0:T(512)S(1)} %bitcast.221), kind=kCustom, calls=%fused_computation.11 | custom fusion | flops 512 | bytes 10240 | tf_op jit(solution)/shard_map/scatter-add | solution.py:112
  408.8 9.5 %all-to-all-start.1 = ((f32[16,1,8192]{2,1,0:T(1,128)}), f32[16,1,8192]{2,1,0:T(1,128)S(1)}, u32[]{:S(2)}, u32[]{:S(2)}) async-start(f32[16,1,8192]{2,1,0:T(1,128)} %reshape.253), calls=%async_computation.1 | async-start | bytes 1048576 | tf_op jit(solution)/shard_map/all_to_all | solution.py:142
  418.4 75.7 %all-reduce.10.cloned.1.call-done = f32[32,32,128]{2,1,0:T(8,128)} async-done(((f32[32,32,128]{2,1,0:T(8,128)}), f32[32,32,128]{2,1,0:T(8,128)}) %all-reduce.10.cloned.1.call-update) | async-done | bytes 524304 | tf_op jit(solution)/shard_map/psum | solution.py:139
  498.7 10.7 %all-to-all-start = ((f32[16,1,8192]{2,1,0:T(1,128)}), f32[16,1,8192]{2,1,0:T(1,128)}, u32[]{:S(2)}, u32[]{:S(2)}) async-start(f32[16,1,8192]{2,1,0:T(1,128)} %reshape.255), calls=%async_computation | async-start | bytes 1048576 | tf_op jit(solution)/shard_map/all_to_all | solution.py:141
  518.2 4.8 convolution_multiply_fusion
  531.9 4.8 fusion.4
  536.8 5.1 convolution_bitcast_fusion
  544.4 6.0 %all-to-all-start.2 = ((f32[16,1,8192]{2,1,0:T(1,128)}), f32[16,1,8192]{2,1,0:T(1,128)S(1)}, u32[]{:S(2)}, u32[]{:S(2)}) async-start(f32[16,1,8192]{2,1,0:T(1,128)} %reshape.257), calls=%async_computation.2 | async-start | bytes 1048576 | tf_op jit(solution)/shard_map/all_to_all | solution.py:145
  550.8 9.5 %all-to-all-done.2 = f32[16,1,8192]{2,1,0:T(1,128)S(1)} async-done(((f32[16,1,8192]{2,1,0:T(1,128)}), f32[16,1,8192]{2,1,0:T(1,128)S(1)}, u32[]{:S(2)}, u32[]{:S(2)}) %all-to-all-start.2) | async-done | bytes 524320 | tf_op jit(solution)/shard_map/all_to_all | solution.py:145
  (226 shorter events, 182.4 us)
Async XLA Ops:
  6.5 487.5 %all-reduce.10.cloned.1.call-start = ((), (), s32[]{:S(2)}) async-start(), calls=%async_computation.3 | async-start | bytes 1048576 | tf_op jit(solution)/shard_map/psum | solution.py:139
  7.5 22.4 %collective-permute-start.3 = (f32[2,4,32,128]{3,2,1,0:T(8,128)S(1)}, f32[2,4,32,128]{3,2,1,0:T(8,128)S(1)}, u32[]{:S(2)}, u32[]{:S(2)}) collective-permute-start(f32[2,4,32,128]{3,2,1,0:T(8,128)S(1)} %get-tuple-element.46), channel_id=1, source_target_pairs={{0,1},{1,2},{2,3},{3,4},{4,5},{5,6},{6,7},{7,8},{8,9},{9,10},{10,1... | collective-permute-start | bytes 393224 | tf_op jit(solution)/shard_map/ppermute | solution.py:17
  12.1 21.3 %collective-permute-start.2 = (f32[2,4,32,128]{3,2,1,0:T(8,128)S(1)}, f32[2,4,32,128]{3,2,1,0:T(8,128)}, u32[]{:S(2)}, u32[]{:S(2)}) collective-permute-start(f32[2,4,32,128]{3,2,1,0:T(8,128)S(1)} %get-tuple-element.47), channel_id=1, source_target_pairs={{1,0},{2,1},{3,2},{4,3},{5,4},{6,5},{7,6},{8,7},{9,8},{10,9},{11,1... | collective-permute-start | bytes 393224 | tf_op jit(solution)/shard_map/ppermute | solution.py:20
  15.7 40.3 %collective-permute-start.1 = (f32[2,4,32,128]{3,2,1,0:T(8,128)}, f32[2,4,32,128]{3,2,1,0:T(8,128)S(1)}, u32[]{:S(2)}, u32[]{:S(2)}) collective-permute-start(f32[2,4,32,128]{3,2,1,0:T(8,128)} %get-tuple-element.50), channel_id=1, source_target_pairs={{0,1},{1,2},{2,3},{3,4},{4,5},{5,6},{6,7},{7,8},{8,9},{9,10},{10,1... | collective-permute-start | bytes 393224 | tf_op jit(solution)/shard_map/ppermute | solution.py:17
  19.4 36.7 %collective-permute-start = (f32[2,4,32,128]{3,2,1,0:T(8,128)}, f32[2,4,32,128]{3,2,1,0:T(8,128)S(1)}, u32[]{:S(2)}, u32[]{:S(2)}) collective-permute-start(f32[2,4,32,128]{3,2,1,0:T(8,128)} %get-tuple-element.51), channel_id=1, source_target_pairs={{1,0},{2,1},{3,2},{4,3},{5,4},{6,5},{7,6},{8,7},{9,8},{10,9},{11,1... | collective-permute-start | bytes 393224 | tf_op jit(solution)/shard_map/ppermute | solution.py:20
  49.7 10.9 %collective-permute-start.5 = (f32[2,4,32,128]{3,2,1,0:T(8,128)S(1)}, f32[2,4,32,128]{3,2,1,0:T(8,128)S(1)}, u32[]{:S(2)}, u32[]{:S(2)}) collective-permute-start(f32[2,4,32,128]{3,2,1,0:T(8,128)S(1)} %get-tuple-element.42), channel_id=1, source_target_pairs={{0,1},{1,2},{2,3},{3,4},{4,5},{5,6},{6,7},{7,8},{8,9},{9,10},{10,1... | collective-permute-start | bytes 393224 | tf_op jit(solution)/shard_map/ppermute | solution.py:17
  53.6 9.3 %collective-permute-start.4 = (f32[2,4,32,128]{3,2,1,0:T(8,128)S(1)}, f32[2,4,32,128]{3,2,1,0:T(8,128)S(1)}, u32[]{:S(2)}, u32[]{:S(2)}) collective-permute-start(f32[2,4,32,128]{3,2,1,0:T(8,128)S(1)} %get-tuple-element.43), channel_id=1, source_target_pairs={{1,0},{2,1},{3,2},{4,3},{5,4},{6,5},{7,6},{8,7},{9,8},{10,9},{11,1... | collective-permute-start | bytes 393224 | tf_op jit(solution)/shard_map/ppermute | solution.py:20
  97.2 22.8 %collective-permute-start.7 = (f32[2,4,32,128]{3,2,1,0:T(8,128)}, f32[2,4,32,128]{3,2,1,0:T(8,128)S(1)}, u32[]{:S(2)}, u32[]{:S(2)}) collective-permute-start(f32[2,4,32,128]{3,2,1,0:T(8,128)} %get-tuple-element.38), channel_id=1, source_target_pairs={{0,1},{1,2},{2,3},{3,4},{4,5},{5,6},{6,7},{7,8},{8,9},{9,10},{10,1... | collective-permute-start | bytes 393224 | tf_op jit(solution)/shard_map/ppermute | solution.py:17
  117.9 6.3 %collective-permute-start.6 = (f32[2,4,32,128]{3,2,1,0:T(8,128)S(1)}, f32[2,4,32,128]{3,2,1,0:T(8,128)S(1)}, u32[]{:S(2)}, u32[]{:S(2)}) collective-permute-start(f32[2,4,32,128]{3,2,1,0:T(8,128)S(1)} %get-tuple-element.39), channel_id=1, source_target_pairs={{1,0},{2,1},{3,2},{4,3},{5,4},{6,5},{7,6},{8,7},{9,8},{10,9},{11,1... | collective-permute-start | bytes 393224 | tf_op jit(solution)/shard_map/ppermute | solution.py:20
  139.2 19.1 %collective-permute-start.9 = (f32[2,4,32,128]{3,2,1,0:T(8,128)S(1)}, f32[2,4,32,128]{3,2,1,0:T(8,128)S(1)}, u32[]{:S(2)}, u32[]{:S(2)}) collective-permute-start(f32[2,4,32,128]{3,2,1,0:T(8,128)S(1)} %get-tuple-element.34), channel_id=1, source_target_pairs={{0,1},{1,2},{2,3},{3,4},{4,5},{5,6},{6,7},{7,8},{8,9},{9,10},{10,1... | collective-permute-start | bytes 393224 | tf_op jit(solution)/shard_map/ppermute | solution.py:17
  155.7 6.3 %collective-permute-start.8 = (f32[2,4,32,128]{3,2,1,0:T(8,128)S(1)}, f32[2,4,32,128]{3,2,1,0:T(8,128)S(1)}, u32[]{:S(2)}, u32[]{:S(2)}) collective-permute-start(f32[2,4,32,128]{3,2,1,0:T(8,128)S(1)} %get-tuple-element.35), channel_id=1, source_target_pairs={{1,0},{2,1},{3,2},{4,3},{5,4},{6,5},{7,6},{8,7},{9,8},{10,9},{11,1... | collective-permute-start | bytes 393224 | tf_op jit(solution)/shard_map/ppermute | solution.py:20
  206.7 4.4 collective-permute-start.11
  208.6 8.4 %collective-permute-start.10 = (f32[2,4,32,128]{3,2,1,0:T(8,128)S(1)}, f32[2,4,32,128]{3,2,1,0:T(8,128)S(1)}, u32[]{:S(2)}, u32[]{:S(2)}) collective-permute-start(f32[2,4,32,128]{3,2,1,0:T(8,128)S(1)} %get-tuple-element.31), channel_id=1, source_target_pairs={{1,0},{2,1},{3,2},{4,3},{5,4},{6,5},{7,6},{8,7},{9,8},{10,9},{11,1... | collective-permute-start | bytes 393224 | tf_op jit(solution)/shard_map/ppermute | solution.py:20
  253.9 4.8 collective-permute-start.13
  255.8 12.4 %collective-permute-start.12 = (f32[2,4,32,128]{3,2,1,0:T(8,128)S(1)}, f32[2,4,32,128]{3,2,1,0:T(8,128)S(1)}, u32[]{:S(2)}, u32[]{:S(2)}) collective-permute-start(f32[2,4,32,128]{3,2,1,0:T(8,128)S(1)} %get-tuple-element.27), channel_id=1, source_target_pairs={{1,0},{2,1},{3,2},{4,3},{5,4},{6,5},{7,6},{8,7},{9,8},{10,9},{11,1... | collective-permute-start | bytes 393224 | tf_op jit(solution)/shard_map/ppermute | solution.py:20
  280.1 26.9 %copy-start.33 = (f32[1,2,2,128]{3,2,1,0:T(2,128)S(1)}, f32[1,2,2,128]{3,2,1,0:T(2,128)}, u32[]{:S(2)}) copy-start(f32[1,2,2,128]{3,2,1,0:T(2,128)} %get-tuple-element.10) | copy-start | bytes 6148
  305.0 4.4 collective-permute-start.15
  307.1 8.3 %collective-permute-start.14 = (f32[2,4,32,128]{3,2,1,0:T(8,128)S(1)}, f32[2,4,32,128]{3,2,1,0:T(8,128)S(1)}, u32[]{:S(2)}, u32[]{:S(2)}) collective-permute-start(f32[2,4,32,128]{3,2,1,0:T(8,128)S(1)} %get-tuple-element.23), channel_id=1, source_target_pairs={{1,0},{2,1},{3,2},{4,3},{5,4},{6,5},{7,6},{8,7},{9,8},{10,9},{11,1... | collective-permute-start | bytes 393224 | tf_op jit(solution)/shard_map/ppermute | solution.py:20
  328.4 71.5 %copy-start.5 = (f32[1,2,1024,128]{3,2,1,0:T(8,128)S(1)}, f32[1,2,1024,128]{3,2,1,0:T(8,128)}, u32[]{:S(2)}) copy-start(f32[1,2,1024,128]{3,2,1,0:T(8,128)} %copy-done.3) | copy-start | bytes 3145732
  328.4 71.5 %copy-start.8 = (f32[1,2,1024,128]{3,2,1,0:T(8,128)S(1)}, f32[1,2,1024,128]{3,2,1,0:T(8,128)}, u32[]{:S(2)}) copy-start(f32[1,2,1024,128]{3,2,1,0:T(8,128)} %copy-done.6) | copy-start | bytes 3145732
  328.4 71.5 %copy-start.10 = (f32[1,2,1024,128]{3,2,1,0:T(8,128)S(1)}, f32[1,2,1024,128]{3,2,1,0:T(8,128)}, u32[]{:S(2)}) copy-start(f32[1,2,1024,128]{3,2,1,0:T(8,128)} %copy-done.9) | copy-start | bytes 3145732
  408.8 89.8 %all-to-all-start.1 = ((f32[16,1,8192]{2,1,0:T(1,128)}), f32[16,1,8192]{2,1,0:T(1,128)S(1)}, u32[]{:S(2)}, u32[]{:S(2)}) async-start(f32[16,1,8192]{2,1,0:T(1,128)} %reshape.253), calls=%async_computation.1 | async-start | bytes 1048576 | tf_op jit(solution)/shard_map/all_to_all | solution.py:142
  498.7 24.4 %all-to-all-start = ((f32[16,1,8192]{2,1,0:T(1,128)}), f32[16,1,8192]{2,1,0:T(1,128)}, u32[]{:S(2)}, u32[]{:S(2)}) async-start(f32[16,1,8192]{2,1,0:T(1,128)} %reshape.255), calls=%async_computation | async-start | bytes 1048576 | tf_op jit(solution)/shard_map/all_to_all | solution.py:141
  544.4 15.9 %all-to-all-start.2 = ((f32[16,1,8192]{2,1,0:T(1,128)}), f32[16,1,8192]{2,1,0:T(1,128)S(1)}, u32[]{:S(2)}, u32[]{:S(2)}) async-start(f32[16,1,8192]{2,1,0:T(1,128)} %reshape.257), calls=%async_computation.2 | async-start | bytes 1048576 | tf_op jit(solution)/shard_map/all_to_all | solution.py:145
  (37 other events, 276.7 us)
Sparse Core Ops, SparseCore 0:
  404.4 89.6 all-reduce.9
where the time goes:
time: 578 us; the launch traced here: 571 us
  other arithmetic  264 us (46%)
  local copies, waits for them, and re-layouts  105 us (18%)
  waiting for transfers between devices  103 us (18%)
  starting transfers between devices  68.8 us (12%)
  between operations  15.5 us (3%)
  matrix products  14.7 us (3%)
    scatter-add x8, other arithmetic, place(): flat.at[rows_full, target].add(values, mode='drop').reshape(field.shape)  151 us
    psum x1, waiting for transfers between devices, body(): total = lax.psum(partial_value, 'shot')  75.7 us
    unnamed x127, local copies, waits for them, and re-layouts  52 us
    add x4, other arithmetic, body(): advanced = 2.0 * current - prior + speed_sq * spread  47.2 us
    add x4, other arithmetic, body(): earlier = 2.0 * adj_current - adj_later + speed_sq * spread  31.4 us
    ppermute x8, starting transfers between devices, extended(): lax.ppermute(lax.slice_in_dim(block, block.shape[dim] - width, None, axis...  24 us
    gather x8, local copies, waits for them, and re-layouts, body(): jnp.take_along_axis(advanced.reshape(shots_here, -1), record_clip, axis=1)  23.5 us
    ppermute x8, starting transfers between devices, extended(): lax.ppermute(lax.slice_in_dim(block, 0, width, axis=dim), axis, backward)  18.6 us
  transfers between devices with their start and end apart: 20, of which 7 were waited for; matrix products, arithmetic and copies ran while one was open for 17% of the time, Pallas kernels for 0%

commit v1 on v0

--- a/solution.py
+++ b/solution.py
@@ -136,7 +136,8 @@
     rate = step_size[0]
     shot_rows = velocity.shape[2] // lax.axis_size("shot")
     start = lax.axis_index("shot") * shot_rows
-    total = lax.psum(partial_value, "shot")
+    terms = lax.all_gather(partial_value, "shot")
+    total = jnp.sum(terms, axis=0)
     grad_cols, noise_cols = (
         lax.all_to_all(total, "dom", split_axis=2, concat_axis=0, tiled=True),
         lax.all_to_all(noise_field, "dom", split_axis=2, concat_axis=0, tiled=True),

time: 578 us -> 564 us (0.976)
  waiting for transfers between devices: 103 us -> 92.4 us
    psum x1 -> x0, waiting for transfers between devices: 75.7 us -> none  [body(): total = lax.psum(partial_value, 'shot')]
    all_gather x0 -> x1, waiting for transfers between devices: none -> 64.8 us  [body(): terms = lax.all_gather(partial_value, 'shot')]
where the time goes in v1:
time: 564 us; the launch traced here: 557 us
  other arithmetic  267 us (47%)
  local copies, waits for them, and re-layouts  104 us (18%)
  waiting for transfers between devices  92.4 us (16%)
  starting transfers between devices  63.9 us (11%)
  between operations  15.5 us (3%)
  matrix products  14.7 us (3%)
    scatter-add x8, other arithmetic, place(): flat.at[rows_full, target].add(values, mode='drop').reshape(field.shape)  151 us
    all_gather x1, waiting for transfers between devices, body(): terms = lax.all_gather(partial_value, 'shot')  64.8 us
    unnamed x127, local copies, waits for them, and re-layouts  52 us
    add x4, other arithmetic, body(): advanced = 2.0 * current - prior + speed_sq * spread  47.2 us
    add x4, other arithmetic, body(): earlier = 2.0 * adj_current - adj_later + speed_sq * spread  31.4 us
    ppermute x8, starting transfers between devices, extended(): lax.ppermute(lax.slice_in_dim(block, block.shape[dim] - width, None, axis...  24 us
    gather x8, local copies, waits for them, and re-layouts, body(): jnp.take_along_axis(advanced.reshape(shots_here, -1), record_clip, axis=1)  23.5 us
    ppermute x8, starting transfers between devices, extended(): lax.ppermute(lax.slice_in_dim(block, 0, width, axis=dim), axis, backward)  18.6 us
  transfers between devices with their start and end apart: 20, of which 7 were waited for; matrix products, arithmetic and copies ran while one was open for 17% of the time, Pallas kernels for 0%

profile of v1, /device:TPU:1, one launch (start us, length us, event | category | flops | bytes accessed | tf_op | source)
XLA Modules:
  0.0 556.8 jit_solution(459686251768567726)
XLA Ops:
  37.4 8.3 %multiply_add_fusion.3 = (f32[2,32,32,128]{3,2,1,0:T(8,128)}, f32[2,32,32,128]{3,2,1,0:T(8,128)}) fusion(f32[2,32,32,128]{3,2,1,0:T(8,128)} %param.17, f32[2,32,32,128]{3,2,1,0:T(8,128)} %param.18, f32[32,32,128]{2,1,0:T(8,128)} %multiply_multiply_fusion, f32[2,40,40,136]{3,2,1,0:T(8,128)S(1)} %select_maximum_fusion.12, f32[2,36,32,128]{3,2,1,0:T(8,128)} %copy-done.23, ...), kind=kLoop, calls=%fused_computation.293 | loop fusion | flops 8650752 | bytes 29884416 | tf_op jit(solution)/shard_map/add | solution.py:122
  66.2 22.5 %multiply_add_fusion.2 = (f32[2,32,32,128]{3,2,1,0:T(8,128)}, f32[2,32,32,128]{3,2,1,0:T(8,128)}) fusion(f32[2,32,32,128]{3,2,1,0:T(8,128)} %param.18, f32[2,32,32,128]{3,2,1,0:T(8,128)} %bitcast.180, f32[32,32,128]{2,1,0:T(8,128)} %multiply_multiply_fusion, f32[2,40,40,136]{3,2,1,0:T(8,128)} %select_maximum_fusion.10, ...), kind=kLoop, calls=%fused_computation.292 | loop fusion | flops 8650752 | bytes 29884416 | tf_op jit(solution)/shard_map/add | solution.py:122
  101.3 7.9 %fusion.75 = f32[2,32,32,128]{3,2,1,0:T(8,128)} fusion(f32[2,40,40,136]{3,2,1,0:T(8,128)S(1)} %select_maximum_fusion.14, f32[2,36,32,128]{3,2,1,0:T(8,128)} %copy-done.22, f32[2,36,32,128]{3,2,1,0:T(8,128)} %constant_dynamic-update-slice_fusion, f32[2,32,32,128]{3,2,1,0:T(8,128)S(1)} %copy-done.18, f32[2,32,32,128]{3,2,1,0:T(8,128)} %param.19, ...), kind=kLoop, calls=%fused_computation.263 | loop fusion | flops 8650752 | bytes 28835840 | tf_op jit(solution)/shard_map/add | solution.py:131
  112.4 4.8 gather_fusion.3
  127.4 8.2 %multiply_add_fusion.1 = (f32[2,32,32,128]{3,2,1,0:T(8,128)}, f32[2,32,32,128]{3,2,1,0:T(8,128)}) fusion(f32[2,32,32,128]{3,2,1,0:T(8,128)} %bitcast.181, f32[2,32,32,128]{3,2,1,0:T(8,128)} %bitcast.184, f32[32,32,128]{2,1,0:T(8,128)} %multiply_multiply_fusion, f32[2,40,40,136]{3,2,1,0:T(8,128)S(1)} %select_maximum_fusion.8, ...), kind=kLoop, calls=%fused_computation.291 | loop fusion | flops 8650752 | bytes 29884416 | tf_op jit(solution)/shard_map/add | solution.py:122
  142.4 7.1 %gather_fusion.2 = f32[512]{0:T(512)} fusion(f32[2,131072]{1,0:T(2,128)S(1)} %copy-done.16, s32[512]{0:T(512)S(1)} %bitcast.157), kind=kCustom, calls=%fused_computation.2.clone | custom fusion | bytes 8192 | tf_op jit(solution)/shard_map/jit(take_along_axis)/gather | solution.py:124
  165.1 8.2 %multiply_add_fusion = (f32[2,32,32,128]{3,2,1,0:T(8,128)}, f32[2,32,32,128]{3,2,1,0:T(8,128)}) fusion(f32[2,32,32,128]{3,2,1,0:T(8,128)} %bitcast.185, f32[2,32,32,128]{3,2,1,0:T(8,128)} %bitcast.196, f32[32,32,128]{2,1,0:T(8,128)} %multiply_multiply_fusion, f32[2,40,40,136]{3,2,1,0:T(8,128)S(1)} %select_maximum_fusion.6, ...), kind=kLoop, calls=%fused_computation.290 | loop fusion | flops 8650752 | bytes 29884416 | tf_op jit(solution)/shard_map/add | solution.py:122
  176.9 4.8 gather_fusion
  181.8 24.7 %scatter_fusion.4 = f32[2,131072]{1,0:T(2,128)S(1)} fusion(f32[2,131072]{1,0:T(2,128)S(1)} %bitcast.197, s32[512]{0:T(512)S(1)} %bitcast.152, f32[512]{0:T(512)S(1)} %bitcast.226), kind=kCustom, calls=%fused_computation.8 | custom fusion | flops 512 | bytes 10240 | tf_op jit(solution)/shard_map/scatter-add | solution.py:112
  219.1 7.8 %fusion.33 = f32[2,32,32,128]{3,2,1,0:T(8,128)} fusion(f32[2,40,40,136]{3,2,1,0:T(8,128)S(1)} %select_maximum_fusion.4, f32[2,36,32,128]{3,2,1,0:T(8,128)} %copy-done.26, f32[2,36,32,128]{3,2,1,0:T(8,128)} %constant_dynamic-update-slice_fusion.20, f32[2,32,32,128]{3,2,1,0:T(8,128)S(1)} %bitcast.163, f32[2,32,32,128]{3,2,1,0:T(8,128)} %param.20, ...), kind=kLoop, calls=%fused_computation.121 | loop fusion | flops 8650752 | bytes 28835840 | tf_op jit(solution)/shard_map/add | solution.py:131
  229.0 24.7 %scatter_fusion.5 = f32[2,131072]{1,0:T(2,128)S(1)} fusion(f32[2,131072]{1,0:T(2,128)S(1)} %bitcast.202, s32[512]{0:T(512)S(1)} %bitcast.153, f32[512]{0:T(512)S(1)} %bitcast.224), kind=kCustom, calls=%fused_computation.9 | custom fusion | flops 512 | bytes 10240 | tf_op jit(solution)/shard_map/scatter-add | solution.py:112
  260.9 7.2 %collective-permute-done.12 = f32[2,4,32,128]{3,2,1,0:T(8,128)S(1)} collective-permute-done((f32[2,4,32,128]{3,2,1,0:T(8,128)S(1)}, f32[2,4,32,128]{3,2,1,0:T(8,128)S(1)}, u32[]{:S(2)}, u32[]{:S(2)}) %collective-permute-start.12) | collective-permute-done | bytes 131104 | tf_op jit(solution)/shard_map/ppermute | solution.py:20
  270.3 7.8 %fusion.23 = f32[2,32,32,128]{3,2,1,0:T(8,128)} fusion(f32[2,40,40,136]{3,2,1,0:T(8,128)S(1)} %select_maximum_fusion.2, f32[2,36,32,128]{3,2,1,0:T(8,128)} %copy-done.27, f32[2,36,32,128]{3,2,1,0:T(8,128)} %constant_dynamic-update-slice_fusion.24, f32[2,32,32,128]{3,2,1,0:T(8,128)} %bitcast.169, f32[2,32,32,128]{3,2,1,0:T(8,128)S(1)} %bitcast.164, ...), kind=kLoop, calls=%fused_computation.91 | loop fusion | flops 8650752 | bytes 28835840 | tf_op jit(solution)/shard_map/add | solution.py:131
  280.1 24.7 %scatter_fusion.6 = f32[2,131072]{1,0:T(2,128)S(1)} fusion(f32[2,131072]{1,0:T(2,128)S(1)} %bitcast.204, s32[512]{0:T(512)S(1)} %bitcast.154, f32[512]{0:T(512)S(1)} %bitcast.225), kind=kCustom, calls=%fused_computation.10 | custom fusion | flops 512 | bytes 10240 | tf_op jit(solution)/shard_map/scatter-add | solution.py:112
  317.5 7.9 %fusion.13 = f32[2,32,32,128]{3,2,1,0:T(8,128)} fusion(f32[2,40,40,136]{3,2,1,0:T(8,128)S(1)} %select_maximum_fusion, f32[2,36,32,128]{3,2,1,0:T(8,128)} %copy-done.28, f32[2,36,32,128]{3,2,1,0:T(8,128)} %constant_dynamic-update-slice_fusion.28, f32[2,32,32,128]{3,2,1,0:T(8,128)} %bitcast.175, f32[2,32,32,128]{3,2,1,0:T(8,128)S(1)} %bitcast.170, ...), kind=kLoop, calls=%fused_computation.61 | loop fusion | flops 8650752 | bytes 28835840 | tf_op jit(solution)/shard_map/add | solution.py:131
  328.4 70.2 %scatter_fusion.7 = f32[2,131072]{1,0:T(2,128)} fusion(f32[2,131072]{1,0:T(2,128)} %bitcast.200, s32[512]{0:T(512)S(1)} %bitcast.155, f32[512]{0:T(512)S(1)} %bitcast.223), kind=kCustom, calls=%fused_computation.11 | custom fusion | flops 512 | bytes 10240 | tf_op jit(solution)/shard_map/scatter-add | solution.py:112
  408.9 9.5 %all-to-all-start.1 = ((f32[16,1,8192]{2,1,0:T(1,128)}), f32[16,1,8192]{2,1,0:T(1,128)S(1)}, u32[]{:S(2)}, u32[]{:S(2)}) async-start(f32[16,1,8192]{2,1,0:T(1,128)} %reshape.254), calls=%async_computation.1 | async-start | bytes 1048576 | tf_op jit(solution)/shard_map/all_to_all | solution.py:143
  418.4 64.8 %all-gather.3.cloned.1.call-done = f32[256,32,128]{2,1,0:T(8,128)} async-done(((f32[32,32,128]{2,1,0:T(8,128)}), f32[256,32,128]{2,1,0:T(8,128)}) %all-gather.3.cloned.1.call-update) | async-done | bytes 4194320 | tf_op jit(solution)/shard_map/all_gather | solution.py:139
  489.4 5.8 %all-to-all-start = ((f32[16,1,8192]{2,1,0:T(1,128)}), f32[16,1,8192]{2,1,0:T(1,128)}, u32[]{:S(2)}, u32[]{:S(2)}) async-start(f32[16,1,8192]{2,1,0:T(1,128)} %reshape.256), calls=%async_computation | async-start | bytes 1048576 | tf_op jit(solution)/shard_map/all_to_all | solution.py:142
  504.1 4.8 convolution_multiply_fusion
  517.8 4.8 fusion.4
  522.6 5.1 convolution_bitcast_fusion
  530.3 6.0 %all-to-all-start.2 = ((f32[16,1,8192]{2,1,0:T(1,128)}), f32[16,1,8192]{2,1,0:T(1,128)S(1)}, u32[]{:S(2)}, u32[]{:S(2)}) async-start(f32[16,1,8192]{2,1,0:T(1,128)} %reshape.258), calls=%async_computation.2 | async-start | bytes 1048576 | tf_op jit(solution)/shard_map/all_to_all | solution.py:146
  536.6 9.5 %all-to-all-done.2 = f32[16,1,8192]{2,1,0:T(1,128)S(1)} async-done(((f32[16,1,8192]{2,1,0:T(1,128)}), f32[16,1,8192]{2,1,0:T(1,128)S(1)}, u32[]{:S(2)}, u32[]{:S(2)}) %all-to-all-start.2) | async-done | bytes 524320 | tf_op jit(solution)/shard_map/all_to_all | solution.py:146
  (227 shorter events, 184.1 us)
Async XLA Ops:
  6.5 476.6 %all-gather.3.cloned.1.call-start = ((), (), s32[]{:S(2)}) async-start(), calls=%async_computation.3 | async-start | bytes 4718592 | tf_op jit(solution)/shard_map/all_gather | solution.py:139
  7.5 22.4 %collective-permute-start.3 = (f32[2,4,32,128]{3,2,1,0:T(8,128)S(1)}, f32[2,4,32,128]{3,2,1,0:T(8,128)S(1)}, u32[]{:S(2)}, u32[]{:S(2)}) collective-permute-start(f32[2,4,32,128]{3,2,1,0:T(8,128)S(1)} %get-tuple-element.46), channel_id=1, source_target_pairs={{0,1},{1,2},{2,3},{3,4},{4,5},{5,6},{6,7},{7,8},{8,9},{9,10},{10,1... | collective-permute-start | bytes 393224 | tf_op jit(solution)/shard_map/ppermute | solution.py:17
  12.1 21.3 %collective-permute-start.2 = (f32[2,4,32,128]{3,2,1,0:T(8,128)S(1)}, f32[2,4,32,128]{3,2,1,0:T(8,128)}, u32[]{:S(2)}, u32[]{:S(2)}) collective-permute-start(f32[2,4,32,128]{3,2,1,0:T(8,128)S(1)} %get-tuple-element.47), channel_id=1, source_target_pairs={{1,0},{2,1},{3,2},{4,3},{5,4},{6,5},{7,6},{8,7},{9,8},{10,9},{11,1... | collective-permute-start | bytes 393224 | tf_op jit(solution)/shard_map/ppermute | solution.py:20
  15.7 40.3 %collective-permute-start.1 = (f32[2,4,32,128]{3,2,1,0:T(8,128)}, f32[2,4,32,128]{3,2,1,0:T(8,128)S(1)}, u32[]{:S(2)}, u32[]{:S(2)}) collective-permute-start(f32[2,4,32,128]{3,2,1,0:T(8,128)} %get-tuple-element.50), channel_id=1, source_target_pairs={{0,1},{1,2},{2,3},{3,4},{4,5},{5,6},{6,7},{7,8},{8,9},{9,10},{10,1... | collective-permute-start | bytes 393224 | tf_op jit(solution)/shard_map/ppermute | solution.py:17
  19.4 36.7 %collective-permute-start = (f32[2,4,32,128]{3,2,1,0:T(8,128)}, f32[2,4,32,128]{3,2,1,0:T(8,128)S(1)}, u32[]{:S(2)}, u32[]{:S(2)}) collective-permute-start(f32[2,4,32,128]{3,2,1,0:T(8,128)} %get-tuple-element.51), channel_id=1, source_target_pairs={{1,0},{2,1},{3,2},{4,3},{5,4},{6,5},{7,6},{8,7},{9,8},{10,9},{11,1... | collective-permute-start | bytes 393224 | tf_op jit(solution)/shard_map/ppermute | solution.py:20
  49.7 10.9 %collective-permute-start.5 = (f32[2,4,32,128]{3,2,1,0:T(8,128)S(1)}, f32[2,4,32,128]{3,2,1,0:T(8,128)S(1)}, u32[]{:S(2)}, u32[]{:S(2)}) collective-permute-start(f32[2,4,32,128]{3,2,1,0:T(8,128)S(1)} %get-tuple-element.42), channel_id=1, source_target_pairs={{0,1},{1,2},{2,3},{3,4},{4,5},{5,6},{6,7},{7,8},{8,9},{9,10},{10,1... | collective-permute-start | bytes 393224 | tf_op jit(solution)/shard_map/ppermute | solution.py:17
  53.6 9.3 %collective-permute-start.4 = (f32[2,4,32,128]{3,2,1,0:T(8,128)S(1)}, f32[2,4,32,128]{3,2,1,0:T(8,128)S(1)}, u32[]{:S(2)}, u32[]{:S(2)}) collective-permute-start(f32[2,4,32,128]{3,2,1,0:T(8,128)S(1)} %get-tuple-element.43), channel_id=1, source_target_pairs={{1,0},{2,1},{3,2},{4,3},{5,4},{6,5},{7,6},{8,7},{9,8},{10,9},{11,1... | collective-permute-start | bytes 393224 | tf_op jit(solution)/shard_map/ppermute | solution.py:20
  97.2 22.8 %collective-permute-start.7 = (f32[2,4,32,128]{3,2,1,0:T(8,128)}, f32[2,4,32,128]{3,2,1,0:T(8,128)S(1)}, u32[]{:S(2)}, u32[]{:S(2)}) collective-permute-start(f32[2,4,32,128]{3,2,1,0:T(8,128)} %get-tuple-element.38), channel_id=1, source_target_pairs={{0,1},{1,2},{2,3},{3,4},{4,5},{5,6},{6,7},{7,8},{8,9},{9,10},{10,1... | collective-permute-start | bytes 393224 | tf_op jit(solution)/shard_map/ppermute | solution.py:17
  117.9 6.3 %collective-permute-start.6 = (f32[2,4,32,128]{3,2,1,0:T(8,128)S(1)}, f32[2,4,32,128]{3,2,1,0:T(8,128)S(1)}, u32[]{:S(2)}, u32[]{:S(2)}) collective-permute-start(f32[2,4,32,128]{3,2,1,0:T(8,128)S(1)} %get-tuple-element.39), channel_id=1, source_target_pairs={{1,0},{2,1},{3,2},{4,3},{5,4},{6,5},{7,6},{8,7},{9,8},{10,9},{11,1... | collective-permute-start | bytes 393224 | tf_op jit(solution)/shard_map/ppermute | solution.py:20
  139.2 19.1 %collective-permute-start.9 = (f32[2,4,32,128]{3,2,1,0:T(8,128)S(1)}, f32[2,4,32,128]{3,2,1,0:T(8,128)S(1)}, u32[]{:S(2)}, u32[]{:S(2)}) collective-permute-start(f32[2,4,32,128]{3,2,1,0:T(8,128)S(1)} %get-tuple-element.34), channel_id=1, source_target_pairs={{0,1},{1,2},{2,3},{3,4},{4,5},{5,6},{6,7},{7,8},{8,9},{9,10},{10,1... | collective-permute-start | bytes 393224 | tf_op jit(solution)/shard_map/ppermute | solution.py:17
  155.7 6.3 %collective-permute-start.8 = (f32[2,4,32,128]{3,2,1,0:T(8,128)S(1)}, f32[2,4,32,128]{3,2,1,0:T(8,128)S(1)}, u32[]{:S(2)}, u32[]{:S(2)}) collective-permute-start(f32[2,4,32,128]{3,2,1,0:T(8,128)S(1)} %get-tuple-element.35), channel_id=1, source_target_pairs={{1,0},{2,1},{3,2},{4,3},{5,4},{6,5},{7,6},{8,7},{9,8},{10,9},{11,1... | collective-permute-start | bytes 393224 | tf_op jit(solution)/shard_map/ppermute | solution.py:20
  206.7 4.4 collective-permute-start.11
  208.6 8.4 %collective-permute-start.10 = (f32[2,4,32,128]{3,2,1,0:T(8,128)S(1)}, f32[2,4,32,128]{3,2,1,0:T(8,128)S(1)}, u32[]{:S(2)}, u32[]{:S(2)}) collective-permute-start(f32[2,4,32,128]{3,2,1,0:T(8,128)S(1)} %get-tuple-element.31), channel_id=1, source_target_pairs={{1,0},{2,1},{3,2},{4,3},{5,4},{6,5},{7,6},{8,7},{9,8},{10,9},{11,1... | collective-permute-start | bytes 393224 | tf_op jit(solution)/shard_map/ppermute | solution.py:20
  253.9 4.8 collective-permute-start.13
  255.8 12.4 %collective-permute-start.12 = (f32[2,4,32,128]{3,2,1,0:T(8,128)S(1)}, f32[2,4,32,128]{3,2,1,0:T(8,128)S(1)}, u32[]{:S(2)}, u32[]{:S(2)}) collective-permute-start(f32[2,4,32,128]{3,2,1,0:T(8,128)S(1)} %get-tuple-element.27), channel_id=1, source_target_pairs={{1,0},{2,1},{3,2},{4,3},{5,4},{6,5},{7,6},{8,7},{9,8},{10,9},{11,1... | collective-permute-start | bytes 393224 | tf_op jit(solution)/shard_map/ppermute | solution.py:20
  280.1 26.9 %copy-start.33 = (f32[1,2,2,128]{3,2,1,0:T(2,128)S(1)}, f32[1,2,2,128]{3,2,1,0:T(2,128)}, u32[]{:S(2)}) copy-start(f32[1,2,2,128]{3,2,1,0:T(2,128)} %get-tuple-element.10) | copy-start | bytes 6148
  305.0 4.4 collective-permute-start.15
  307.1 8.3 %collective-permute-start.14 = (f32[2,4,32,128]{3,2,1,0:T(8,128)S(1)}, f32[2,4,32,128]{3,2,1,0:T(8,128)S(1)}, u32[]{:S(2)}, u32[]{:S(2)}) collective-permute-start(f32[2,4,32,128]{3,2,1,0:T(8,128)S(1)} %get-tuple-element.23), channel_id=1, source_target_pairs={{1,0},{2,1},{3,2},{4,3},{5,4},{6,5},{7,6},{8,7},{9,8},{10,9},{11,1... | collective-permute-start | bytes 393224 | tf_op jit(solution)/shard_map/ppermute | solution.py:20
  328.4 71.5 %copy-start.5 = (f32[1,2,1024,128]{3,2,1,0:T(8,128)S(1)}, f32[1,2,1024,128]{3,2,1,0:T(8,128)}, u32[]{:S(2)}) copy-start(f32[1,2,1024,128]{3,2,1,0:T(8,128)} %copy-done.3) | copy-start | bytes 3145732
  328.4 71.5 %copy-start.8 = (f32[1,2,1024,128]{3,2,1,0:T(8,128)S(1)}, f32[1,2,1024,128]{3,2,1,0:T(8,128)}, u32[]{:S(2)}) copy-start(f32[1,2,1024,128]{3,2,1,0:T(8,128)} %copy-done.6) | copy-start | bytes 3145732
  328.4 71.5 %copy-start.10 = (f32[1,2,1024,128]{3,2,1,0:T(8,128)S(1)}, f32[1,2,1024,128]{3,2,1,0:T(8,128)}, u32[]{:S(2)}) copy-start(f32[1,2,1024,128]{3,2,1,0:T(8,128)} %copy-done.9) | copy-start | bytes 3145732
  408.9 80.6 %all-to-all-start.1 = ((f32[16,1,8192]{2,1,0:T(1,128)}), f32[16,1,8192]{2,1,0:T(1,128)S(1)}, u32[]{:S(2)}, u32[]{:S(2)}) async-start(f32[16,1,8192]{2,1,0:T(1,128)} %reshape.254), calls=%async_computation.1 | async-start | bytes 1048576 | tf_op jit(solution)/shard_map/all_to_all | solution.py:143
  489.4 19.5 %all-to-all-start = ((f32[16,1,8192]{2,1,0:T(1,128)}), f32[16,1,8192]{2,1,0:T(1,128)}, u32[]{:S(2)}, u32[]{:S(2)}) async-start(f32[16,1,8192]{2,1,0:T(1,128)} %reshape.256), calls=%async_computation | async-start | bytes 1048576 | tf_op jit(solution)/shard_map/all_to_all | solution.py:142
  530.3 15.9 %all-to-all-start.2 = ((f32[16,1,8192]{2,1,0:T(1,128)}), f32[16,1,8192]{2,1,0:T(1,128)S(1)}, u32[]{:S(2)}, u32[]{:S(2)}) async-start(f32[16,1,8192]{2,1,0:T(1,128)} %reshape.258), calls=%async_computation.2 | async-start | bytes 1048576 | tf_op jit(solution)/shard_map/all_to_all | solution.py:146
  (37 other events, 276.7 us)
Sparse Core Ops, SparseCore 0:
  404.4 78.7 all-gather.2
